TPU v7x, 256 devices: a whole 4x4x8 slice. The times are simulated.
256 devices in a mesh: gx: 8 (over x, core), gy: 4 (over z_lo), gz: 8 (over y, z_hi).
Axes of the slice: x: 4, y: 4, z: 8 (z_hi: 2, z_lo: 4; z = z_hi * 4 + z_lo), core: 2. Of those that a mesh axis runs over, the one named last changes fastest.
Arguments:
- start_block: float32 [32, 3, 2, 8, 16, 1024], P(None, None, None, 'gx', 'gy', 'gz'), may hold values from -700 to 700
- pair_blocks: float32 [3, 3, 16, 2, 8, 16, 1024], P(None, None, None, None, 'gx', 'gy', 'gz'), may hold values from -8 to 8, as said below
- slot_map: int32 [16, 2, 8, 16, 1024], P(None, None, 'gx', 'gy', 'gz'), may hold values from 0 to 15, as said below
Outputs:
- alpha1: float32 [32, 32], replicated
- alpha2: float32 [32, 32], replicated
- beta1: float32 [32, 32], replicated
- beta2: float32 [32, 32], replicated
- basis3: float32 [32, 3, 2, 8, 16, 1024], P(None, None, None, 'gx', 'gy', 'gz')
Inputs may be any that keep to these rules, and one draw needn't show every extreme that they name: `slot_map`: for every atom the 16 slots hold each of 0 to 15 once; 0 to 13 name the neighbour directions of the steps, 14 and 15 mark padding slots. `pair_blocks`: the block an atom holds toward a neighbour is the transpose of the block that neighbour holds toward the atom, so H is symmetric.
All inputs are finite; a program needn't handle non-finite values.
Results may differ from a plain program's by a relative error of at most 0.0003.
Values sent between devices are 32-bit elements; how exact they have to be, the bound alone decides.
A program may use at most 64 MiB of HBM per device.

v0:
```python
import jax
import jax.numpy as jnp
from jax import lax
from jax.sharding import PartitionSpec as P

PRECISE = lax.Precision.HIGHEST


def extended(block, sides, width):
    for axis, dim in sides:
        count = lax.axis_size(axis)
        forward = [(i, i + 1) for i in range(count - 1)]
        forward.append((count - 1, 0))
        backward = [(target, source) for source, target in forward]
        low = lax.ppermute(
            lax.slice_in_dim(block, block.shape[dim] - width, None, axis=dim), axis, forward
        )
        high = lax.ppermute(lax.slice_in_dim(block, 0, width, axis=dim), axis, backward)
        block = jnp.concatenate([low, block, high], axis=dim)
    return block


def neighbour_offset(sublattice, offset_id):
    if offset_id < 8:
        corner_bits = (offset_id >> 2 & 1, offset_id >> 1 & 1, offset_id & 1)
        if sublattice == 0:
            return ((-corner_bits[0], -corner_bits[1], -corner_bits[2]), 1)
        return (corner_bits, 0)
    axis_id = (offset_id - 8) // 2
    direction = 1 if (offset_id - 8) % 2 == 0 else -1
    displacement = tuple((direction if axis_number == axis_id else 0 for axis_number in range(3)))
    return (displacement, sublattice)


def offset_blocks(pair_blocks, slot_map):
    result = []
    for offset_id in range(14):
        chosen = slot_map[None, None] == offset_id
        result.append(jnp.sum(jnp.where(chosen, pair_blocks, jnp.float32(0.0)), axis=2))
    return result


def onsite_blocks(blocks):
    result = []
    for sublattice in range(2):
        onsite = jnp.zeros(blocks[0].shape[:2] + blocks[0].shape[3:], jnp.float32)
        for offset_id in range(14):
            coupling = blocks[offset_id][:, :, sublattice]
            onsite = onsite + 0.5 * (coupling + jnp.swapaxes(coupling, 0, 1))
        result.append(onsite)
    return result


def apply_hessian(vectors, blocks, onsite):
    padded = extended(vectors, (("gx", 3), ("gy", 4), ("gz", 5)), 1)
    size_x, size_y, size_z = (vectors.shape[3], vectors.shape[4], vectors.shape[5])
    outputs = []
    for sublattice in range(2):
        summed = jnp.zeros(vectors.shape[:2] + vectors.shape[3:], jnp.float32)
        for offset_id in range(14):
            displacement, source = neighbour_offset(sublattice, offset_id)
            start_x = 1 + displacement[0]
            start_y = 1 + displacement[1]
            start_z = 1 + displacement[2]
            neighbour = padded[
                :,
                :,
                source,
                start_x : start_x + size_x,
                start_y : start_y + size_y,
                start_z : start_z + size_z,
            ]
            coupling = blocks[offset_id][:, :, sublattice]
            summed = summed + jnp.sum(coupling[None] * neighbour[:, None], axis=2)
        summed = summed - jnp.sum(
            onsite[sublattice][None] * vectors[:, None, :, sublattice], axis=2
        )
        outputs.append(summed)
    return jnp.stack(outputs, axis=2)


def local_gram(left, right):
    left_flat = left.reshape(left.shape[0], -1)
    right_flat = right.reshape(right.shape[0], -1)
    return lax.dot_general(left_flat, right_flat, (((1,), (1,)), ((), ())), precision=PRECISE)


def combine(matrix, vectors):
    flat = vectors.reshape(vectors.shape[0], -1)
    return jnp.dot(matrix, flat, precision=PRECISE).reshape(vectors.shape)


def inverse_factor(gram_matrix):
    lower = jnp.linalg.cholesky(gram_matrix)
    identity = jnp.eye(gram_matrix.shape[0], dtype=gram_matrix.dtype)
    inverse = jax.scipy.linalg.solve_triangular(lower, identity, lower=True)
    return (lower, inverse)


def lanczos_step(basis, image, previous, coupling_prev, row_count):
    alpha = lax.psum(local_gram(image, basis), ("gx", "gy", "gz")) / row_count
    residual = image - combine(alpha, basis)
    if previous is not None:
        residual = residual - combine(coupling_prev.T, previous)
    residual_gram = lax.psum(local_gram(residual, residual), ("gx", "gy", "gz")) / row_count
    return (alpha, residual, residual_gram)


def local(start_block, pair_blocks, slot_map):
    device_count = lax.axis_size("gx") * lax.axis_size("gy") * lax.axis_size("gz")
    row_count = start_block[0].size * device_count
    blocks = offset_blocks(pair_blocks, slot_map)
    onsite = onsite_blocks(blocks)
    start_gram = lax.psum(local_gram(start_block, start_block), ("gx", "gy", "gz")) / row_count
    lower0, inverse0 = inverse_factor(start_gram)
    basis1 = combine(inverse0, start_block)
    image1 = apply_hessian(basis1, blocks, onsite)
    alpha1, residual1, gram_first = lanczos_step(basis1, image1, None, None, row_count)
    beta1, inverse1 = inverse_factor(gram_first)
    basis2 = combine(inverse1, residual1)
    image2 = apply_hessian(basis2, blocks, onsite)
    alpha2, residual2, gram_second = lanczos_step(basis2, image2, basis1, beta1, row_count)
    beta2, inverse2 = inverse_factor(gram_second)
    basis3 = combine(inverse2, residual2)
    return (alpha1, alpha2, beta1, beta2, basis3)


def solution(mesh):
    in_specs = (
        P(None, None, None, "gx", "gy", "gz"),
        P(None, None, None, None, "gx", "gy", "gz"),
        P(None, None, "gx", "gy", "gz"),
    )
    out_specs = (P(), P(), P(), P(), P(None, None, None, "gx", "gy", "gz"))
    return jax.shard_map(local, mesh=mesh, in_specs=in_specs, out_specs=out_specs, check_vma=False)
```

profile of v0, /device:TPU:1, one launch (start us, length us, event | category | flops | bytes accessed | tf_op | source)
XLA Modules:
  0.0 522.5 jit_solution(3226206658296597986)
XLA Ops:
  0.6 1.2 reshape.1549
  1.8 1.6 convolution_bitcast_fusion.2
  3.4 81.5 %psum.35 = f32[32,32]{0,1:T(8,128)S(1)} all-reduce(f32[32,32]{0,1:T(8,128)S(1)} %convolution_bitcast_fusion.2), channel_id=1, replica_groups=mesh['gx'=8,'gy'=4,'gz'=8] {'gx','gy','gz'}, use_global_device_ids=true, to_apply=%region_1.2 | all-reduce | flops 1024 | bytes 8192 | tf_op jit(solution)/shard_map/psum | solution.py:114
  85.0 2.9 cholesky.59
  88.6 0.7 fusion.44
  89.3 2.4 custom-call.7
  92.8 1.0 collective-permute-start.1
  94.1 2.5 select_reduce_fusion.13
  103.9 0.8 multiply_reduce_fusion.45
  104.7 0.8 multiply_reduce_fusion.59
  106.4 2.7 collective-permute-start.3
  109.2 0.7 slice_bitcast_fusion.9
  109.9 0.7 multiply_reduce_fusion.50
  110.6 0.9 multiply_reduce_fusion.55
  111.5 0.9 multiply_reduce_fusion.51
  112.3 1.1 collective-permute-done.2
  113.4 6.9 %collective-permute-done.3 = f32[32,3,2,3,1,128]{5,0,4,3,2,1:T(8,128)S(1)} collective-permute-done((f32[32,3,2,3,1,128]{5,0,4,3,2,1:T(8,128)S(1)}, f32[32,3,2,3,1,128]{5,0,4,3,2,1:T(8,128)S(1)}, u32[]{:S(2)}, u32[]{:S(2)}) %collective-permute-start.3) | collective-permute-done | bytes 294944 | tf_op jit(solution)/shard_map/ppermute | solution.py:18
  120.3 0.7 copy-done.10
  121.2 1.8 fusion.52
  123.1 2.8 copy.507
  125.9 5.6 %collective-permute-start.5 = (f32[32,3,2,3,6,1]{0,2,5,4,3,1:T(2,128)}, f32[32,3,2,3,6,1]{0,2,5,4,3,1:T(2,128)}, u32[]{:S(2)}, u32[]{:S(2)}) collective-permute-start(f32[32,3,2,3,6,1]{0,2,5,4,3,1:T(2,128)} %copy.507), channel_id=1, source_target_pairs={{1,0},{2,1},{3,2},{4,3},{5,4},{6,5},{7,6},{0,7},{9,8},{10,9},{11,1... | collective-permute-start | bytes 41480 | tf_op jit(solution)/shard_map/ppermute | solution.py:18
  131.5 1.3 copy.506
  132.8 1.7 multiply_reduce_fusion.36
  134.5 2.7 copy.419
  137.2 5.0 collective-permute-done.4
  142.2 1.5 copy.395
  143.8 1.4 fusion.8
  151.0 74.3 %psum.36 = f32[32,32]{0,1:T(8,128)S(1)} all-reduce(f32[32,32]{0,1:T(8,128)S(1)} %fusion.56), channel_id=1, replica_groups=mesh['gx'=8,'gy'=4,'gz'=8] {'gx','gy','gz'}, use_global_device_ids=true, to_apply=%region_47.50 | all-reduce | flops 1024 | bytes 8192 | tf_op jit(solution)/shard_map/psum | solution.py:101
  226.4 73.7 %psum.37 = f32[32,32]{0,1:T(8,128)S(1)} all-reduce(f32[32,32]{0,1:T(8,128)S(1)} %fusion.57), channel_id=1, replica_groups=mesh['gx'=8,'gy'=4,'gz'=8] {'gx','gy','gz'}, use_global_device_ids=true, to_apply=%region_48.51 | all-reduce | flops 1024 | bytes 8192 | tf_op jit(solution)/shard_map/psum | solution.py:105
  300.2 2.9 cholesky.70
  304.4 2.4 custom-call.8
  307.9 1.2 collective-permute-start.6
  309.2 0.8 multiply_reduce_fusion.15
  310.1 0.8 multiply_reduce_fusion.29
  311.0 0.7 copy.495
  311.7 2.2 collective-permute-done.6
  314.0 2.6 collective-permute-done.7
  316.7 1.0 collective-permute-start.8
  317.7 2.4 collective-permute-start.9
  320.2 0.7 multiply_reduce_fusion.20
  320.9 0.9 multiply_reduce_fusion.25
  321.8 0.9 multiply_reduce_fusion.21
  322.6 4.1 collective-permute-done.8
  326.7 5.3 %collective-permute-done.9 = f32[32,3,2,3,1,128]{5,0,4,3,2,1:T(8,128)S(1)} collective-permute-done((f32[32,3,2,3,1,128]{5,0,4,3,2,1:T(8,128)S(1)}, f32[32,3,2,3,1,128]{5,0,4,3,2,1:T(8,128)S(1)}, u32[]{:S(2)}, u32[]{:S(2)}) %collective-permute-start.9) | collective-permute-done | bytes 294944 | tf_op jit(solution)/shard_map/ppermute | solution.py:18
  332.0 0.7 copy-done.6
  332.9 1.8 fusion.51
  334.8 2.8 copy.509
  337.6 4.7 collective-permute-start.11
  342.2 1.5 multiply_reduce_fusion.6
  343.7 1.3 copy.508
  345.0 0.7 collective-permute-start.10
  345.7 1.5 copy.488
  347.2 2.2 maximum_bitcast_fusion.4
  349.5 0.9 multiply_reduce_fusion.17
  350.4 4.6 collective-permute-done.10
  354.9 1.5 copy.486
  356.5 1.4 fusion.4
  363.7 73.7 %psum.38 = f32[32,32]{0,1:T(8,128)S(1)} all-reduce(f32[32,32]{0,1:T(8,128)S(1)} %fusion.59), channel_id=1, replica_groups=mesh['gx'=8,'gy'=4,'gz'=8] {'gx','gy','gz'}, use_global_device_ids=true, to_apply=%region_79.82 | all-reduce | flops 1024 | bytes 8192 | tf_op jit(solution)/shard_map/psum | solution.py:101
  439.1 73.7 %psum.39 = f32[32,32]{0,1:T(8,128)S(1)} all-reduce(f32[32,32]{0,1:T(8,128)S(1)} %fusion.60), channel_id=1, replica_groups=mesh['gx'=8,'gy'=4,'gz'=8] {'gx','gy','gz'}, use_global_device_ids=true, to_apply=%region_80.83 | all-reduce | flops 1024 | bytes 8192 | tf_op jit(solution)/shard_map/psum | solution.py:105
  512.8 2.9 cholesky.81
  516.4 1.3 select_bitcast_fusion
  517.6 2.4 custom-call.9
  520.8 1.0 copy.497
  521.8 0.7 copy.496
  (321 shorter events, 28.2 us)
Async XLA Ops:
  3.4 90.4 %copy-start.95 = (s32[16,2,1,4,128]{4,3,2,1,0:T(4,128)S(1)}, s32[16,2,1,4,128]{4,3,2,1,0:T(4,128)}, u32[]{:S(2)}) copy-start(s32[16,2,1,4,128]{4,3,2,1,0:T(4,128)} %param.8) | copy-start | bytes 196612
  88.6 5.5 %copy-start.35 = (f32[3,3,16,2,1,4,128]{6,5,4,3,2,1,0:T(4,128)S(1)}, f32[3,3,16,2,1,4,128]{6,5,4,3,2,1,0:T(4,128)}, u32[]{:S(2)}) copy-start(f32[3,3,16,2,1,4,128]{6,5,4,3,2,1,0:T(4,128)} %param.7) | copy-start | bytes 1769476
  92.8 12.8 %collective-permute-start = (f32[32,3,2,1,4,128]{5,0,4,3,2,1:T(8,128)S(1)}, f32[32,3,2,1,4,128]{5,0,4,3,2,1:T(8,128)S(1)}, u32[]{:S(2)}, u32[]{:S(2)}) collective-permute-start(f32[32,3,2,1,4,128]{5,0,4,3,2,1:T(8,128)S(1)} %copy.391), channel_id=1, source_target_pairs={{0,32},{32,64},{64,96},{96,128},{128,160},{160,192},{192,224},{224... | collective-permute-start | bytes 1179656 | tf_op jit(solution)/shard_map/ppermute | solution.py:15
  92.8 12.9 %collective-permute-start.1 = (f32[32,3,2,1,4,128]{5,0,4,3,2,1:T(8,128)S(1)}, f32[32,3,2,1,4,128]{5,0,4,3,2,1:T(8,128)S(1)}, u32[]{:S(2)}, u32[]{:S(2)}) collective-permute-start(f32[32,3,2,1,4,128]{5,0,4,3,2,1:T(8,128)S(1)} %copy.391), channel_id=1, source_target_pairs={{32,0},{64,32},{96,64},{128,96},{160,128},{192,160},{224,192},{0,2... | collective-permute-start | bytes 1179656 | tf_op jit(solution)/shard_map/ppermute | solution.py:18
  99.9 10.0 %copy-start.84 = (f32[3,3,4,128]{3,2,0,1:T(4,128)}, f32[3,3,4,128]{3,2,0,1:T(4,128)S(1)}, u32[]{:S(2)}) copy-start(f32[3,3,4,128]{3,2,0,1:T(4,128)S(1)} %get-tuple-element.159) | copy-start | bytes 55300
  99.9 10.7 %copy-start.82 = (f32[3,3,4,128]{3,2,0,1:T(4,128)}, f32[3,3,4,128]{3,2,0,1:T(4,128)S(1)}, u32[]{:S(2)}) copy-start(f32[3,3,4,128]{3,2,0,1:T(4,128)S(1)} %get-tuple-element.162) | copy-start | bytes 55300
  100.5 10.9 %copy-start.80 = (f32[3,3,4,128]{3,2,0,1:T(4,128)}, f32[3,3,4,128]{3,2,0,1:T(4,128)S(1)}, u32[]{:S(2)}) copy-start(f32[3,3,4,128]{3,2,0,1:T(4,128)S(1)} %get-tuple-element.194) | copy-start | bytes 55300
  102.5 8.1 %copy-start.88 = (f32[3,3,4,128]{3,2,0,1:T(4,128)}, f32[3,3,4,128]{3,2,0,1:T(4,128)S(1)}, u32[]{:S(2)}) copy-start(f32[3,3,4,128]{3,2,0,1:T(4,128)S(1)} %get-tuple-element.190) | copy-start | bytes 55300
  102.5 9.0 %copy-start.86 = (f32[3,3,4,128]{3,2,0,1:T(4,128)}, f32[3,3,4,128]{3,2,0,1:T(4,128)S(1)}, u32[]{:S(2)}) copy-start(f32[3,3,4,128]{3,2,0,1:T(4,128)S(1)} %get-tuple-element.189) | copy-start | bytes 55300
  103.8 1.8 copy-start.90
  103.8 1.8 copy-start.92
  103.9 1.9 copy-start.36
  104.7 1.1 copy-start.38
  105.8 7.6 %collective-permute-start.2 = (f32[32,3,2,3,1,128]{5,0,4,3,2,1:T(8,128)S(1)}, f32[32,3,2,3,1,128]{5,0,4,3,2,1:T(8,128)S(1)}, u32[]{:S(2)}, u32[]{:S(2)}) collective-permute-start(f32[32,3,2,3,1,128]{5,0,4,3,2,1:T(8,128)S(1)} %get-tuple-element.115), channel_id=1, source_target_pairs={{0,8},{8,16},{16,24},{24,0},{1,9},{9,17},{17,25},{25,1},{2,10},{10... | collective-permute-start | bytes 884744 | tf_op jit(solution)/shard_map/ppermute | solution.py:15
  106.4 13.9 %collective-permute-start.3 = (f32[32,3,2,3,1,128]{5,0,4,3,2,1:T(8,128)S(1)}, f32[32,3,2,3,1,128]{5,0,4,3,2,1:T(8,128)S(1)}, u32[]{:S(2)}, u32[]{:S(2)}) collective-permute-start(f32[32,3,2,3,1,128]{5,0,4,3,2,1:T(8,128)S(1)} %get-tuple-element.116), channel_id=1, source_target_pairs={{8,0},{16,8},{24,16},{0,24},{9,1},{17,9},{25,17},{1,25},{10,2},{18... | collective-permute-start | bytes 884744 | tf_op jit(solution)/shard_map/ppermute | solution.py:18
  113.4 6.9 %copy-start.8 = (f32[32,3,2,3,1,128]{5,0,4,3,2,1:T(8,128)}, f32[32,3,2,3,1,128]{5,0,4,3,2,1:T(8,128)S(1)}, u32[]{:S(2)}) copy-start(f32[32,3,2,3,1,128]{5,0,4,3,2,1:T(8,128)S(1)} %collective-permute-done.2) | copy-start | bytes 884740
  125.9 8.6 %collective-permute-start.5 = (f32[32,3,2,3,6,1]{0,2,5,4,3,1:T(2,128)}, f32[32,3,2,3,6,1]{0,2,5,4,3,1:T(2,128)}, u32[]{:S(2)}, u32[]{:S(2)}) collective-permute-start(f32[32,3,2,3,6,1]{0,2,5,4,3,1:T(2,128)} %copy.507), channel_id=1, source_target_pairs={{1,0},{2,1},{3,2},{4,3},{5,4},{6,5},{7,6},{0,7},{9,8},{10,9},{11,1... | collective-permute-start | bytes 41480 | tf_op jit(solution)/shard_map/ppermute | solution.py:18
  132.8 9.4 %collective-permute-start.4 = (f32[32,3,2,3,6,1]{0,2,5,4,3,1:T(2,128)}, f32[32,3,2,3,6,1]{0,2,5,4,3,1:T(2,128)}, u32[]{:S(2)}, u32[]{:S(2)}) collective-permute-start(f32[32,3,2,3,6,1]{0,2,5,4,3,1:T(2,128)} %copy.506), channel_id=1, source_target_pairs={{0,1},{1,2},{2,3},{3,4},{4,5},{5,6},{6,7},{7,0},{8,9},{9,10},{10,1... | collective-permute-start | bytes 41480 | tf_op jit(solution)/shard_map/ppermute | solution.py:15
  143.8 1.4 copy-start.54
  143.8 1.5 copy-start.72
  143.8 1.5 copy-start.9
  143.8 1.5 copy-start.11
  145.4 1.5 copy-start
  147.9 1.1 copy-start.27
  147.9 1.2 copy-start.28
  147.9 1.2 copy-start.33
  148.6 1.1 copy-start.24
  148.6 1.2 copy-start.34
  304.4 133.4 %copy-start.94 = (f32[32,32]{1,0:T(8,128)}, f32[32,32]{1,0:T(8,128)S(1)}, u32[]{:S(2)}) copy-start(f32[32,32]{1,0:T(8,128)S(1)} %get-tuple-element.76) | copy-start | bytes 12292
  307.1 2.1 copy-start.37
  307.1 2.1 copy-start.93
  307.6 2.5 copy-start.2
  307.6 2.5 copy-start.39
  307.6 2.5 copy-start.91
  307.9 5.9 %collective-permute-start.6 = (f32[32,3,2,1,4,128]{5,0,4,3,2,1:T(8,128)S(1)}, f32[32,3,2,1,4,128]{5,0,4,3,2,1:T(8,128)S(1)}, u32[]{:S(2)}, u32[]{:S(2)}) collective-permute-start(f32[32,3,2,1,4,128]{5,0,4,3,2,1:T(8,128)S(1)} %copy.482), channel_id=1, source_target_pairs={{0,32},{32,64},{64,96},{96,128},{128,160},{160,192},{192,224},{224... | collective-permute-start | bytes 1179656 | tf_op jit(solution)/shard_map/ppermute | solution.py:15
  309.1 7.5 %collective-permute-start.7 = (f32[32,3,2,1,4,128]{5,0,4,3,2,1:T(8,128)S(1)}, f32[32,3,2,1,4,128]{5,0,4,3,2,1:T(8,128)S(1)}, u32[]{:S(2)}, u32[]{:S(2)}) collective-permute-start(f32[32,3,2,1,4,128]{5,0,4,3,2,1:T(8,128)S(1)} %copy.482), channel_id=1, source_target_pairs={{32,0},{64,32},{96,64},{128,96},{160,128},{192,160},{224,192},{0,2... | collective-permute-start | bytes 1179656 | tf_op jit(solution)/shard_map/ppermute | solution.py:18
  314.0 6.2 %copy-start.85 = (f32[3,3,4,128]{3,2,0,1:T(4,128)S(1)}, f32[3,3,4,128]{3,2,0,1:T(4,128)}, u32[]{:S(2)}) copy-start(f32[3,3,4,128]{3,2,0,1:T(4,128)} %copy-done.84) | copy-start | bytes 55300
  316.7 4.2 copy-start.83
  316.7 4.2 copy-start.89
  316.7 5.1 copy-start.81
  316.7 5.1 copy-start.87
  316.7 10.0 %collective-permute-start.8 = (f32[32,3,2,3,1,128]{5,0,4,3,2,1:T(8,128)S(1)}, f32[32,3,2,3,1,128]{5,0,4,3,2,1:T(8,128)S(1)}, u32[]{:S(2)}, u32[]{:S(2)}) collective-permute-start(f32[32,3,2,3,1,128]{5,0,4,3,2,1:T(8,128)S(1)} %get-tuple-element.113), channel_id=1, source_target_pairs={{0,8},{8,16},{16,24},{24,0},{1,9},{9,17},{17,25},{25,1},{2,10},{10... | collective-permute-start | bytes 884744 | tf_op jit(solution)/shard_map/ppermute | solution.py:15
  317.7 14.3 %collective-permute-start.9 = (f32[32,3,2,3,1,128]{5,0,4,3,2,1:T(8,128)S(1)}, f32[32,3,2,3,1,128]{5,0,4,3,2,1:T(8,128)S(1)}, u32[]{:S(2)}, u32[]{:S(2)}) collective-permute-start(f32[32,3,2,3,1,128]{5,0,4,3,2,1:T(8,128)S(1)} %get-tuple-element.114), channel_id=1, source_target_pairs={{8,0},{16,8},{24,16},{0,24},{9,1},{17,9},{25,17},{1,25},{10,2},{18... | collective-permute-start | bytes 884744 | tf_op jit(solution)/shard_map/ppermute | solution.py:18
  326.7 5.3 %copy-start.4 = (f32[32,3,2,3,1,128]{5,0,4,3,2,1:T(8,128)}, f32[32,3,2,3,1,128]{5,0,4,3,2,1:T(8,128)S(1)}, u32[]{:S(2)}) copy-start(f32[32,3,2,3,1,128]{5,0,4,3,2,1:T(8,128)S(1)} %collective-permute-done.8) | copy-start | bytes 884740
  337.6 8.1 %collective-permute-start.11 = (f32[32,3,2,3,6,1]{0,2,5,4,3,1:T(2,128)}, f32[32,3,2,3,6,1]{0,2,5,4,3,1:T(2,128)}, u32[]{:S(2)}, u32[]{:S(2)}) collective-permute-start(f32[32,3,2,3,6,1]{0,2,5,4,3,1:T(2,128)} %copy.509), channel_id=1, source_target_pairs={{1,0},{2,1},{3,2},{4,3},{5,4},{6,5},{7,6},{0,7},{9,8},{10,9},{11,1... | collective-permute-start | bytes 41480 | tf_op jit(solution)/shard_map/ppermute | solution.py:18
  345.0 9.9 %collective-permute-start.10 = (f32[32,3,2,3,6,1]{0,2,5,4,3,1:T(2,128)}, f32[32,3,2,3,6,1]{0,2,5,4,3,1:T(2,128)}, u32[]{:S(2)}, u32[]{:S(2)}) collective-permute-start(f32[32,3,2,3,6,1]{0,2,5,4,3,1:T(2,128)} %copy.508), channel_id=1, source_target_pairs={{0,1},{1,2},{2,3},{3,4},{4,5},{5,6},{6,7},{7,0},{8,9},{9,10},{10,1... | collective-permute-start | bytes 41480 | tf_op jit(solution)/shard_map/ppermute | solution.py:15
  347.2 2.2 copy-start.1
  347.2 2.2 copy-start.59
  347.2 2.2 copy-start.63
  356.4 1.4 copy-start.65
  356.5 1.5 copy-start.79
  356.5 1.6 copy-start.55
  356.5 1.6 copy-start.73
  356.5 1.7 copy-start.57
  356.5 1.7 copy-start.77
  359.3 1.1 copy-start.53
  359.9 1.1 copy-start.25
  359.9 1.2 copy-start.26
  359.9 1.2 copy-start.30
  359.9 1.3 copy-start.31
  360.6 1.1 copy-start.21
  360.6 1.2 copy-start.22
  360.6 1.2 copy-start.29
  360.6 1.3 copy-start.32
  (44 other events, 39.3 us)
where the time goes:
time: 524 us; the launch traced here: 522 us
  blocking collectives  377 us (72%)
  other arithmetic  45.5 us (9%)
  local copies, waits for them, and re-layouts  39 us (7%)
  waiting for transfers between devices  31.8 us (6%)
  starting transfers between devices  19.9 us (4%)
  matrix products  7.11 us (1%)
    psum x2, blocking collectives, lanczos_step(): alpha = lax.psum(local_gram(image, basis), ('gx', 'gy', 'gz')) / row_count  148 us
    psum x2, blocking collectives, lanczos_step(): lax.psum(local_gram(residual, residual), ('gx', 'gy', 'gz')) / row_count  147 us
    psum x1, blocking collectives, local(): lax.psum(local_gram(start_block, start_block), ('gx', 'gy', 'gz'))  81.5 us
    unnamed x203, local copies, waits for them, and re-layouts  17 us
    ppermute x6, waiting for transfers between devices, extended(): lax.ppermute(lax.slice_in_dim(block, block.shape[dim] - width, None, axis...  17 us
    ppermute x6, starting transfers between devices, extended(): lax.ppermute(lax.slice_in_dim(block, 0, width, axis=dim), axis, backward)  16.3 us
    ppermute x6, waiting for transfers between devices, extended(): lax.ppermute(lax.slice_in_dim(block, 0, width, axis=dim), axis, backward)  14.8 us
    reduce_sum x42, other arithmetic, apply_hessian(): summed = summed + jnp.sum(coupling[None] * neighbour[:, None], axis=2)  12.5 us
  transfers between devices with their start and end apart: 12, of which 8 were waited for; matrix products, arithmetic and copies ran while one was open for 6% of the time, Pallas kernels for 0%

commit v1 on v0

--- a/solution.py
+++ b/solution.py
@@ -102,7 +102,10 @@
     residual = image - combine(alpha, basis)
     if previous is not None:
         residual = residual - combine(coupling_prev.T, previous)
-    residual_gram = lax.psum(local_gram(residual, residual), ("gx", "gy", "gz")) / row_count
+    residual_gram = (
+        jnp.sum(lax.all_gather(local_gram(residual, residual), ("gx", "gy", "gz")), axis=0)
+        / row_count
+    )
     return (alpha, residual, residual_gram)
 
 

time: 524 us -> 1810 us (3.45)
  waiting for transfers between devices: 31.8 us -> 1430 us
  blocking collectives: 377 us -> 234 us
    all_gather x0 -> x2, waiting for transfers between devices: none -> 1400 us  [lanczos_step(): lax.all_gather(local_gram(residual, residual), ('gx', 'gy', 'gz'))]
    psum x2 -> x0, blocking collectives: 147 us -> none  [lanczos_step(): lax.psum(local_gram(residual, residual), ('gx', 'gy', 'gz')) / row_count]
  transfers between devices with their start and end apart: 12 -> 14, of which waited for: 8 -> 9; matrix products, arithmetic and copies ran while one was open for 6% -> 2% of each run, Pallas kernels for 0% -> 0%
where the time goes in v1:
time: 1810 us; the launch traced here: 1800 us
  waiting for transfers between devices  1430 us (79%)
  blocking collectives  234 us (13%)
  other arithmetic  51.2 us (3%)
  local copies, waits for them, and re-layouts  39.1 us (2%)
  starting transfers between devices  25.8 us (1%)
    all_gather x2, waiting for transfers between devices, lanczos_step(): lax.all_gather(local_gram(residual, residual), ('gx', 'gy', 'gz'))  1400 us
    psum x2, blocking collectives, lanczos_step(): alpha = lax.psum(local_gram(image, basis), ('gx', 'gy', 'gz')) / row_count  152 us
    psum x1, blocking collectives, local(): lax.psum(local_gram(start_block, start_block), ('gx', 'gy', 'gz'))  81.5 us
  transfers between devices with their start and end apart: 14, of which 9 were waited for; matrix products, arithmetic and copies ran while one was open for 2% of the time, Pallas kernels for 0%

profile of v1, /device:TPU:1, one launch (start us, length us, event | category | flops | bytes accessed | tf_op | source)
XLA Modules:
  0.0 1803.2 jit_solution(11848156598074382441)
XLA Ops:
  7.2 1.2 reshape.1549
  8.4 1.6 convolution_bitcast_fusion.2
  10.0 81.5 %psum.21 = f32[32,32]{0,1:T(8,128)S(1)} all-reduce(f32[32,32]{0,1:T(8,128)S(1)} %convolution_bitcast_fusion.2), channel_id=1, replica_groups=mesh['gx'=8,'gy'=4,'gz'=8] {'gx','gy','gz'}, use_global_device_ids=true, to_apply=%region_1.2 | all-reduce | flops 1024 | bytes 8192 | tf_op jit(solution)/shard_map/psum | solution.py:117
  91.6 2.9 cholesky.59
  95.2 0.7 fusion.44
  95.9 2.4 custom-call.7
  99.4 1.0 collective-permute-start.1
  100.7 2.5 select_reduce_fusion.13
  110.5 0.8 multiply_reduce_fusion.45
  111.3 0.8 multiply_reduce_fusion.59
  113.0 2.7 collective-permute-start.3
  116.5 0.7 multiply_reduce_fusion.50
  117.2 0.9 multiply_reduce_fusion.55
  118.0 0.9 multiply_reduce_fusion.51
  118.9 1.1 collective-permute-done.2
  120.0 6.9 collective-permute-done.3
  126.9 0.7 copy-done.10
  127.8 1.8 fusion.52
  129.7 2.8 copy.503
  132.4 5.6 collective-permute-start.5
  138.1 1.3 copy.502
  139.4 1.7 multiply_reduce_fusion.36
  141.0 2.7 copy.417
  143.8 5.0 collective-permute-done.4
  148.8 1.5 copy.393
  150.4 1.4 fusion.8
  157.6 74.4 %psum.22 = f32[32,32]{0,1:T(8,128)S(1)} all-reduce(f32[32,32]{0,1:T(8,128)S(1)} %fusion.56), channel_id=1, replica_groups=mesh['gx'=8,'gy'=4,'gz'=8] {'gx','gy','gz'}, use_global_device_ids=true, to_apply=%region_47.50 | all-reduce | flops 1024 | bytes 8192 | tf_op jit(solution)/shard_map/psum | solution.py:101
  232.5 1.1 fusion.57
  233.7 703.0 %all-gather.5.cloned.1.call-done = f32[8192,32]{1,0:T(8,128)} async-done(((f32[32,32]{1,0:T(8,128)}), f32[8192,32]{1,0:T(8,128)}) %all-gather.5.cloned.1.call-update) | async-done | bytes 1048592 | tf_op jit(solution)/shard_map/all_gather | solution.py:106
  936.7 2.5 reduce_sum.870
  939.4 2.9 cholesky.70
  943.0 1.3 select_bitcast_fusion.1
  944.2 2.4 custom-call.8
  947.7 0.9 collective-permute-start.7
  948.7 0.8 multiply_reduce_fusion.15
  949.6 0.8 multiply_reduce_fusion.29
  950.4 2.0 collective-permute-done.6
  952.6 2.7 collective-permute-done.7
  955.4 3.1 collective-permute-start.8
  958.5 4.7 collective-permute-start.9
  963.3 0.7 multiply_reduce_fusion.20
  964.0 0.9 multiply_reduce_fusion.25
  964.9 0.9 multiply_reduce_fusion.21
  965.7 3.3 collective-permute-done.8
  969.0 3.5 collective-permute-done.9
  972.5 0.7 copy-done.6
  973.4 1.8 fusion.51
  975.3 2.8 copy.505
  978.1 1.5 multiply_reduce_fusion.6
  979.5 1.3 copy.504
  980.8 7.0 collective-permute-start.10
  987.9 1.5 copy.486
  989.4 2.2 maximum_bitcast_fusion.4
  991.7 0.9 multiply_reduce_fusion.17
  992.5 1.5 copy.484
  994.1 1.4 fusion.4
  1001.3 78.0 %psum.23 = f32[32,32]{0,1:T(8,128)S(1)} all-reduce(f32[32,32]{0,1:T(8,128)S(1)} %fusion.59), channel_id=1, replica_groups=mesh['gx'=8,'gy'=4,'gz'=8] {'gx','gy','gz'}, use_global_device_ids=true, to_apply=%region_79.82 | all-reduce | flops 1024 | bytes 8192 | tf_op jit(solution)/shard_map/psum | solution.py:101
  1080.3 1.1 fusion.60
  1083.0 701.6 %all-gather.7.cloned.1.call-done = f32[8192,32]{1,0:T(8,128)} async-done(((f32[32,32]{1,0:T(8,128)}), f32[8192,32]{1,0:T(8,128)}) %all-gather.7.cloned.1.call-update) | async-done | bytes 1048592 | tf_op jit(solution)/shard_map/all_gather | solution.py:106
  1784.6 2.5 reduce_sum.921
  1787.3 2.9 cholesky.81
  1790.9 1.3 select_bitcast_fusion
  1792.1 2.4 custom-call.9
  1795.3 1.0 copy.495
  (329 shorter events, 29.0 us)
Async XLA Ops:
  7.2 929.5 %all-gather.5.cloned.1.call-start = ((), (), s32[]{:S(2)}) async-start(), calls=%async_computation | async-start | bytes 4210688 | tf_op jit(solution)/shard_map/all_gather | solution.py:106
  10.0 90.4 %copy-start.95 = (s32[16,2,1,4,128]{4,3,2,1,0:T(4,128)S(1)}, s32[16,2,1,4,128]{4,3,2,1,0:T(4,128)}, u32[]{:S(2)}) copy-start(s32[16,2,1,4,128]{4,3,2,1,0:T(4,128)} %param.8) | copy-start | bytes 196612
  95.2 5.5 copy-start.35
  99.3 12.8 collective-permute-start
  99.4 12.9 collective-permute-start.1
  106.5 10.0 copy-start.84
  106.5 10.7 copy-start.82
  107.1 10.9 copy-start.80
  109.0 8.1 copy-start.88
  109.1 9.0 copy-start.86
  110.3 1.8 copy-start.90
  110.4 1.8 copy-start.92
  110.5 1.9 copy-start.36
  112.4 7.6 collective-permute-start.2
  113.0 13.9 collective-permute-start.3
  120.0 6.9 copy-start.8
  132.4 8.6 collective-permute-start.5
  139.4 9.4 collective-permute-start.4
  150.3 1.4 copy-start.54
  150.3 1.5 copy-start.72
  150.4 1.5 copy-start.9
  150.4 1.5 copy-start.11
  152.0 1.5 copy-start
  154.5 1.1 copy-start.27
  154.5 1.2 copy-start.28
  154.5 1.2 copy-start.33
  155.2 1.1 copy-start.24
  155.2 1.2 copy-start.34
  233.6 1551.0 %all-gather.7.cloned.1.call-start = ((), (), s32[]{:S(2)}) async-start(), calls=%async_computation.1 | async-start | bytes 4210688 | tf_op jit(solution)/shard_map/all_gather | solution.py:106
  947.4 2.2 copy-start.2
  947.4 1.3 copy-start.37
  947.4 1.3 copy-start.93
  947.4 2.2 copy-start.39
  947.4 2.2 copy-start.91
  947.7 4.7 collective-permute-start.6
  947.7 7.5 collective-permute-start.7
  952.5 10.7 copy-start.85
  955.3 8.7 copy-start.83
  955.3 8.7 copy-start.89
  955.3 9.6 copy-start.81
  955.3 9.6 copy-start.87
  955.4 13.6 collective-permute-start.8
  958.5 14.0 collective-permute-start.9
  969.0 3.5 copy-start.4
  978.0 9.8 collective-permute-start.11
  980.8 11.7 collective-permute-start.10
  989.4 2.2 copy-start.1
  989.4 2.2 copy-start.59
  989.4 2.2 copy-start.63
  994.0 1.4 copy-start.65
  994.1 1.5 copy-start.79
  994.1 1.6 copy-start.55
  994.1 1.6 copy-start.73
  994.1 1.7 copy-start.57
  994.1 1.7 copy-start.77
  996.9 1.1 copy-start.53
  997.5 1.2 copy-start.26
  997.5 1.2 copy-start.30
  997.5 1.3 copy-start.31
  998.2 1.1 copy-start.21
  998.2 1.2 copy-start.22
  998.2 1.2 copy-start.29
  998.2 1.3 copy-start.32
  999.8 80.0 %copy-start.94 = (f32[32,32]{1,0:T(8,128)S(1)}, f32[32,32]{1,0:T(8,128)}, u32[]{:S(2)}) copy-start(f32[32,32]{1,0:T(8,128)} %get-tuple-element.76) | copy-start | bytes 12292
  (46 other events, 41.5 us)
Sparse Core Ops, SparseCore 0:
  233.7 702.8 all-gather.4
  1081.5 703.0 all-gather.6
